TPU v7x, 128 devices: a whole 4x4x4 slice. The times are simulated.
128 devices in a mesh: lon: 32 (over x, z, core), lat: 4 (over y).
Axes of the slice: x: 4, y: 4, z: 4, core: 2. Of those that a mesh axis runs over, the one named last changes fastest.
Arguments:
- obs_values: bfloat16 [16384, 31, 256], P(('lon', 'lat')), may hold values from -6 to 6
- obs_offset: float32 [16384, 2, 256], P(('lon', 'lat')), may hold values from -0.5 to 0.5
- obs_cell: int32 [16384, 256], P(('lon', 'lat')), may hold values from 0 to 511
- obs_slot: int32 [16384, 256], P(('lon', 'lat')), may hold values from 0 to 11
- obs_count: int32 [128, 128], P(('lon', 'lat')), may hold values from 1 to 256, as said below
- embed_weight: bfloat16 [384, 256], replicated, may hold values from -0.3125 to 0.3125
- embed_bias: float32 [256], replicated, may hold values from -3 to 3
- stride_weight: bfloat16 [9, 256, 256], replicated, may hold values from -0.125 to 0.125
- stride_bias: float32 [256], replicated, may hold values from -3 to 3
- depth_weight: float32 [9, 256], replicated, may hold values from -2 to 2
- norm_gain: float32 [256], replicated, may hold values from 0.1 to 1.9
Outputs:
- encoded: bfloat16 [32, 512, 256], P('lat', 'lon')
Inputs may be any that keep to these rules, and one draw needn't show every extreme that they name: `obs_count`: every entry is at least 1; in every draw one destination tile receives exactly 256 live slots from every source shard.
All inputs are finite; a program needn't handle non-finite values.
Results may differ from a plain program's by a relative error of at most 0.011.
Values may be sent and summed in bfloat16 or wider, within the bound.
A program may use at most 128 MiB of HBM per device.

v0:
```python
import jax
import jax.numpy as jnp
from jax import lax
from jax.sharding import PartitionSpec as P

D = 256
OBS_VARS = 31
SLOTS = 12
TLAT = 16
TLON = 32
CELLS = 512


def shifted(value, axis, by):
    size = lax.axis_size(axis)
    pairs = [(i, i + by) for i in range(size) if 0 <= i + by < size]
    return lax.ppermute(value, axis, pairs)


def shifted_2(value, axis, steps):
    count = lax.axis_size(axis)
    pairs = [(source, (source + steps) % count) for source in range(count)]
    return lax.ppermute(value, axis, pairs)


def with_halo(value, sides, width, wrap):
    for axis, dim in sides:
        size, length = (lax.axis_size(axis), value.shape[dim])
        up = [(i, (i + 1) % size) for i in range(size if wrap else size - 1)]
        down = [(j, i) for i, j in up]
        last = lax.slice_in_dim(value, length - width, length, axis=dim)
        leading = lax.slice_in_dim(value, 0, width, axis=dim)
        before = lax.ppermute(last, axis, up)
        after = lax.ppermute(leading, axis, down)
        value = jnp.concatenate([before, value, after], axis=dim)
    return value


def spread_block(total, values, codes):
    slot_of = codes // CELLS
    cell_of = codes - slot_of * CELLS
    cell_hot = (cell_of[None] == lax.broadcasted_iota(jnp.int32, (CELLS,) + codes.shape, 0)).astype(
        jnp.bfloat16
    )
    slot_hot = (slot_of[None] == lax.broadcasted_iota(jnp.int32, (SLOTS,) + codes.shape, 0)).astype(
        jnp.bfloat16
    )
    spread = slot_hot[:, None] * values[None]
    return total + jnp.einsum("cgr,skgr->csk", cell_hot, spread, preferred_element_type=jnp.float32)


def layer_norm(mixed, norm_gain):
    centre = mixed - jnp.mean(mixed, axis=-1, keepdims=True)
    spread = jnp.mean(centre * centre, axis=-1, keepdims=True)
    return centre * lax.rsqrt(spread + 1e-05) * norm_gain


def on_device(
    obs_values,
    obs_offset,
    obs_cell,
    obs_slot,
    obs_count,
    embed_weight,
    embed_bias,
    stride_weight,
    stride_bias,
    depth_weight,
    norm_gain,
):
    lon_count = lax.axis_size("lon")
    lat_count = lax.axis_size("lat")
    tiles = lon_count * lat_count
    capacity = obs_values.shape[2]
    width = OBS_VARS + 1
    position = lax.broadcasted_iota(jnp.int32, obs_cell.shape, 1)
    live = position < obs_count[0][:, None]
    radius = obs_offset[:, 0, :] * obs_offset[:, 0, :] + obs_offset[:, 1, :] * obs_offset[:, 1, :]
    weight = jnp.where(live, jnp.exp(-2.0 * radius), jnp.float32(0.0))
    scaled = obs_values.astype(jnp.float32) * weight[:, None, :]
    packed = jnp.concatenate([scaled, weight[:, None, :]], axis=1).astype(jnp.bfloat16)
    codes = jnp.where(live, obs_slot * CELLS + obs_cell, -1)
    arrived, arrived_codes = (
        lax.all_to_all(packed, ("lon", "lat"), split_axis=0, concat_axis=0, tiled=True),
        lax.all_to_all(codes, ("lon", "lat"), split_axis=0, concat_axis=0, tiled=True),
    )
    rows_step = min(2048, tiles * capacity)
    empty = jnp.zeros((CELLS, SLOTS, width), jnp.float32)
    group = rows_step // capacity

    def step_padded(index, total):
        block_values = lax.dynamic_slice_in_dim(arrived, index * group, group, 0)
        block_codes = lax.dynamic_slice_in_dim(arrived_codes, index * group, group, 0)
        return spread_block(total, jnp.moveaxis(block_values, 1, 0), block_codes)

    total = lax.fori_loop(0, tiles // group, step_padded, empty)
    density = total[:, :, width - 1 :]
    ratio = total[:, :, : width - 1] / (1.0 + density)
    gridded = (
        jnp.concatenate([ratio, density], axis=2).reshape(CELLS, SLOTS * width).astype(jnp.bfloat16)
    )
    projected = jnp.dot(gridded, embed_weight, preferred_element_type=jnp.float32) + embed_bias
    embedded = jax.nn.gelu(projected).astype(jnp.bfloat16).reshape(TLAT, TLON, D)
    upper = shifted(embedded[TLAT - 1 :], "lat", 1)
    taller = jnp.concatenate([upper, embedded], axis=0)
    before = shifted_2(taller[:, TLON - 1 :], "lon", 1)
    framed = jnp.concatenate([before, taller], axis=1)
    patches = jnp.concatenate(
        [
            framed[row_at : row_at + TLAT - 1 : 2, col_at : col_at + TLON - 1 : 2]
            for row_at in range(3)
            for col_at in range(3)
        ],
        axis=2,
    )
    strided = (
        jnp.dot(
            patches.reshape(-1, 9 * D),
            stride_weight.reshape(9 * D, D),
            preferred_element_type=jnp.float32,
        )
        + stride_bias
    )
    coarse = jax.nn.gelu(strided).astype(jnp.bfloat16).reshape(TLAT // 2, TLON // 2, D)
    wide = with_halo(coarse, (("lon", 1),), 1, True)
    full = with_halo(wide, (("lat", 0),), 1, False)
    depth = jnp.zeros((TLAT // 2, TLON // 2, D), jnp.float32)
    for row_at in range(3):
        for col_at in range(3):
            depth = (
                depth
                + full[row_at : row_at + TLAT // 2, col_at : col_at + TLON // 2].astype(jnp.float32)
                * depth_weight[3 * row_at + col_at]
            )
    mixed = coarse.astype(jnp.float32) + depth
    return layer_norm(mixed, norm_gain).astype(jnp.bfloat16)


def solution(mesh):
    placed = (
        P(("lon", "lat"), None, None),
        P(("lon", "lat"), None, None),
        P(("lon", "lat"), None),
        P(("lon", "lat"), None),
        P(("lon", "lat"), None),
        P(),
        P(),
        P(),
        P(),
        P(),
        P(),
    )
    return jax.shard_map(
        on_device, mesh=mesh, in_specs=placed, out_specs=P("lat", "lon", None), check_vma=False
    )
```

profile of v0, /device:TPU:0, one launch (start us, length us, event | category | flops | bytes accessed | tf_op | source)
XLA Modules:
  0.0 154.2 jit_solution(12176542992178373173)
XLA Ops:
  1.9 11.1 %all-to-all-start = ((s32[128,1,256]{2,1,0:T(1,128)}), s32[128,1,256]{2,1,0:T(1,128)S(1)}, u32[]{:S(2)}, u32[]{:S(2)}) async-start(s32[128,1,256]{2,1,0:T(1,128)} %all_to_all.11), calls=%async_computation | async-start | bytes 262144 | tf_op jit(solution)/shard_map/all_to_all | solution.py:85
  19.4 3.1 %all-to-all-done = s32[128,1,256]{2,1,0:T(1,128)S(1)} async-done(((s32[128,1,256]{2,1,0:T(1,128)}), s32[128,1,256]{2,1,0:T(1,128)S(1)}, u32[]{:S(2)}, u32[]{:S(2)}) %all-to-all-start) | async-done | bytes 131104 | tf_op jit(solution)/shard_map/all_to_all | solution.py:85
  22.5 6.7 %all-to-all-start.1 = ((bf16[128,32,256]{2,1,0:T(8,128)(2,1)}), bf16[128,32,256]{2,1,0:T(8,128)(2,1)S(1)}, u32[]{:S(2)}, u32[]{:S(2)}) async-start(bf16[128,32,256]{2,1,0:T(8,128)(2,1)} %pad_maximum_fusion), calls=%async_computation.1 | async-start | bytes 4194304 | tf_op jit(solution)/shard_map/all_to_all | solution.py:84
  29.8 29.5 %all-to-all-done.1 = bf16[128,32,256]{2,1,0:T(8,128)(2,1)S(1)} async-done(((bf16[128,32,256]{2,1,0:T(8,128)(2,1)}), bf16[128,32,256]{2,1,0:T(8,128)(2,1)S(1)}, u32[]{:S(2)}, u32[]{:S(2)}) %all-to-all-start.1) | async-done | bytes 2097184 | tf_op jit(solution)/shard_map/all_to_all | solution.py:84
  59.3 61.5 %while.16 = (s32[]{:T(128)}, f32[512,12,32]{0,2,1:T(8,128)}, s32[128,256]{1,0:T(8,128)}, bf16[128,32,256]{2,1,0:T(8,128)(2,1)S(1)}, s32[]{:T(128)}, /*index=5*/s32[]{:T(128)}, s32[]{:T(128)}, s32[]{:T(128)}) while((s32[]{:T(128)}, f32[512,12,32]{0,2,1:T(8,128)}, s32[128,256]{1,0:T(8,128)}, bf16[128,32,256]{2,1,0:T(8,128)(2,1)S(1)}, ...), condition=%wide.region_1.2_spmd.clone, body=%wide.region_0.1_spmd.clone.sunk | while | flops 809977856 | bytes 2105493 | solution.py:96
  62.8 3.2 %fusion.57 = f32[512,12,32]{0,2,1:T(8,128)} fusion(s32[8,256]{1,0:T(8,128)S(1)} %get-tuple-element.188, f32[512,12,32]{0,2,1:T(8,128)} %get-tuple-element.199, bf16[32,8,256]{2,0,1:T(8,128)(2,1)S(1)} %dynamic-slice_bitcast_fusion.2, bf16[12,8,256]{2,1,0:T(8,128)(2,1)S(1)} %fusion.56, pred[]{:T(512)S(6)} %compare.13), kind=kOutput, calls=%fused_computation.6.clone.1 | convolution fusion | flops 809893888 | bytes 1761281 | tf_op jit(solution)/shard_map/while/body/eval_jaxpr/cgr,skgr->csk/dot_general | solution.py:49
  66.7 3.2 %fusion.57 = f32[512,12,32]{0,2,1:T(8,128)} fusion(s32[8,256]{1,0:T(8,128)S(1)} %get-tuple-element.188, f32[512,12,32]{0,2,1:T(8,128)} %get-tuple-element.199, bf16[32,8,256]{2,0,1:T(8,128)(2,1)S(1)} %dynamic-slice_bitcast_fusion.2, bf16[12,8,256]{2,1,0:T(8,128)(2,1)S(1)} %fusion.56, pred[]{:T(512)S(6)} %compare.13), kind=kOutput, calls=%fused_computation.6.clone.1 | convolution fusion | flops 809893888 | bytes 1761281 | tf_op jit(solution)/shard_map/while/body/eval_jaxpr/cgr,skgr->csk/dot_general | solution.py:49
  70.7 3.2 %fusion.57 = f32[512,12,32]{0,2,1:T(8,128)} fusion(s32[8,256]{1,0:T(8,128)S(1)} %get-tuple-element.188, f32[512,12,32]{0,2,1:T(8,128)} %get-tuple-element.199, bf16[32,8,256]{2,0,1:T(8,128)(2,1)S(1)} %dynamic-slice_bitcast_fusion.2, bf16[12,8,256]{2,1,0:T(8,128)(2,1)S(1)} %fusion.56, pred[]{:T(512)S(6)} %compare.13), kind=kOutput, calls=%fused_computation.6.clone.1 | convolution fusion | flops 809893888 | bytes 1761281 | tf_op jit(solution)/shard_map/while/body/eval_jaxpr/cgr,skgr->csk/dot_general | solution.py:49
  74.6 3.2 %fusion.57 = f32[512,12,32]{0,2,1:T(8,128)} fusion(s32[8,256]{1,0:T(8,128)S(1)} %get-tuple-element.188, f32[512,12,32]{0,2,1:T(8,128)} %get-tuple-element.199, bf16[32,8,256]{2,0,1:T(8,128)(2,1)S(1)} %dynamic-slice_bitcast_fusion.2, bf16[12,8,256]{2,1,0:T(8,128)(2,1)S(1)} %fusion.56, pred[]{:T(512)S(6)} %compare.13), kind=kOutput, calls=%fused_computation.6.clone.1 | convolution fusion | flops 809893888 | bytes 1761281 | tf_op jit(solution)/shard_map/while/body/eval_jaxpr/cgr,skgr->csk/dot_general | solution.py:49
  78.5 3.2 %fusion.57 = f32[512,12,32]{0,2,1:T(8,128)} fusion(s32[8,256]{1,0:T(8,128)S(1)} %get-tuple-element.188, f32[512,12,32]{0,2,1:T(8,128)} %get-tuple-element.199, bf16[32,8,256]{2,0,1:T(8,128)(2,1)S(1)} %dynamic-slice_bitcast_fusion.2, bf16[12,8,256]{2,1,0:T(8,128)(2,1)S(1)} %fusion.56, pred[]{:T(512)S(6)} %compare.13), kind=kOutput, calls=%fused_computation.6.clone.1 | convolution fusion | flops 809893888 | bytes 1761281 | tf_op jit(solution)/shard_map/while/body/eval_jaxpr/cgr,skgr->csk/dot_general | solution.py:49
  82.4 3.2 %fusion.57 = f32[512,12,32]{0,2,1:T(8,128)} fusion(s32[8,256]{1,0:T(8,128)S(1)} %get-tuple-element.188, f32[512,12,32]{0,2,1:T(8,128)} %get-tuple-element.199, bf16[32,8,256]{2,0,1:T(8,128)(2,1)S(1)} %dynamic-slice_bitcast_fusion.2, bf16[12,8,256]{2,1,0:T(8,128)(2,1)S(1)} %fusion.56, pred[]{:T(512)S(6)} %compare.13), kind=kOutput, calls=%fused_computation.6.clone.1 | convolution fusion | flops 809893888 | bytes 1761281 | tf_op jit(solution)/shard_map/while/body/eval_jaxpr/cgr,skgr->csk/dot_general | solution.py:49
  86.3 3.2 %fusion.57 = f32[512,12,32]{0,2,1:T(8,128)} fusion(s32[8,256]{1,0:T(8,128)S(1)} %get-tuple-element.188, f32[512,12,32]{0,2,1:T(8,128)} %get-tuple-element.199, bf16[32,8,256]{2,0,1:T(8,128)(2,1)S(1)} %dynamic-slice_bitcast_fusion.2, bf16[12,8,256]{2,1,0:T(8,128)(2,1)S(1)} %fusion.56, pred[]{:T(512)S(6)} %compare.13), kind=kOutput, calls=%fused_computation.6.clone.1 | convolution fusion | flops 809893888 | bytes 1761281 | tf_op jit(solution)/shard_map/while/body/eval_jaxpr/cgr,skgr->csk/dot_general | solution.py:49
  90.2 3.2 %fusion.57 = f32[512,12,32]{0,2,1:T(8,128)} fusion(s32[8,256]{1,0:T(8,128)S(1)} %get-tuple-element.188, f32[512,12,32]{0,2,1:T(8,128)} %get-tuple-element.199, bf16[32,8,256]{2,0,1:T(8,128)(2,1)S(1)} %dynamic-slice_bitcast_fusion.2, bf16[12,8,256]{2,1,0:T(8,128)(2,1)S(1)} %fusion.56, pred[]{:T(512)S(6)} %compare.13), kind=kOutput, calls=%fused_computation.6.clone.1 | convolution fusion | flops 809893888 | bytes 1761281 | tf_op jit(solution)/shard_map/while/body/eval_jaxpr/cgr,skgr->csk/dot_general | solution.py:49
  94.2 3.2 %fusion.57 = f32[512,12,32]{0,2,1:T(8,128)} fusion(s32[8,256]{1,0:T(8,128)S(1)} %get-tuple-element.188, f32[512,12,32]{0,2,1:T(8,128)} %get-tuple-element.199, bf16[32,8,256]{2,0,1:T(8,128)(2,1)S(1)} %dynamic-slice_bitcast_fusion.2, bf16[12,8,256]{2,1,0:T(8,128)(2,1)S(1)} %fusion.56, pred[]{:T(512)S(6)} %compare.13), kind=kOutput, calls=%fused_computation.6.clone.1 | convolution fusion | flops 809893888 | bytes 1761281 | tf_op jit(solution)/shard_map/while/body/eval_jaxpr/cgr,skgr->csk/dot_general | solution.py:49
  98.1 3.2 %fusion.57 = f32[512,12,32]{0,2,1:T(8,128)} fusion(s32[8,256]{1,0:T(8,128)S(1)} %get-tuple-element.188, f32[512,12,32]{0,2,1:T(8,128)} %get-tuple-element.199, bf16[32,8,256]{2,0,1:T(8,128)(2,1)S(1)} %dynamic-slice_bitcast_fusion.2, bf16[12,8,256]{2,1,0:T(8,128)(2,1)S(1)} %fusion.56, pred[]{:T(512)S(6)} %compare.13), kind=kOutput, calls=%fused_computation.6.clone.1 | convolution fusion | flops 809893888 | bytes 1761281 | tf_op jit(solution)/shard_map/while/body/eval_jaxpr/cgr,skgr->csk/dot_general | solution.py:49
  102.0 3.2 %fusion.57 = f32[512,12,32]{0,2,1:T(8,128)} fusion(s32[8,256]{1,0:T(8,128)S(1)} %get-tuple-element.188, f32[512,12,32]{0,2,1:T(8,128)} %get-tuple-element.199, bf16[32,8,256]{2,0,1:T(8,128)(2,1)S(1)} %dynamic-slice_bitcast_fusion.2, bf16[12,8,256]{2,1,0:T(8,128)(2,1)S(1)} %fusion.56, pred[]{:T(512)S(6)} %compare.13), kind=kOutput, calls=%fused_computation.6.clone.1 | convolution fusion | flops 809893888 | bytes 1761281 | tf_op jit(solution)/shard_map/while/body/eval_jaxpr/cgr,skgr->csk/dot_general | solution.py:49
  105.9 3.2 %fusion.57 = f32[512,12,32]{0,2,1:T(8,128)} fusion(s32[8,256]{1,0:T(8,128)S(1)} %get-tuple-element.188, f32[512,12,32]{0,2,1:T(8,128)} %get-tuple-element.199, bf16[32,8,256]{2,0,1:T(8,128)(2,1)S(1)} %dynamic-slice_bitcast_fusion.2, bf16[12,8,256]{2,1,0:T(8,128)(2,1)S(1)} %fusion.56, pred[]{:T(512)S(6)} %compare.13), kind=kOutput, calls=%fused_computation.6.clone.1 | convolution fusion | flops 809893888 | bytes 1761281 | tf_op jit(solution)/shard_map/while/body/eval_jaxpr/cgr,skgr->csk/dot_general | solution.py:49
  109.8 3.2 %fusion.57 = f32[512,12,32]{0,2,1:T(8,128)} fusion(s32[8,256]{1,0:T(8,128)S(1)} %get-tuple-element.188, f32[512,12,32]{0,2,1:T(8,128)} %get-tuple-element.199, bf16[32,8,256]{2,0,1:T(8,128)(2,1)S(1)} %dynamic-slice_bitcast_fusion.2, bf16[12,8,256]{2,1,0:T(8,128)(2,1)S(1)} %fusion.56, pred[]{:T(512)S(6)} %compare.13), kind=kOutput, calls=%fused_computation.6.clone.1 | convolution fusion | flops 809893888 | bytes 1761281 | tf_op jit(solution)/shard_map/while/body/eval_jaxpr/cgr,skgr->csk/dot_general | solution.py:49
  113.7 3.2 %fusion.57 = f32[512,12,32]{0,2,1:T(8,128)} fusion(s32[8,256]{1,0:T(8,128)S(1)} %get-tuple-element.188, f32[512,12,32]{0,2,1:T(8,128)} %get-tuple-element.199, bf16[32,8,256]{2,0,1:T(8,128)(2,1)S(1)} %dynamic-slice_bitcast_fusion.2, bf16[12,8,256]{2,1,0:T(8,128)(2,1)S(1)} %fusion.56, pred[]{:T(512)S(6)} %compare.13), kind=kOutput, calls=%fused_computation.6.clone.1 | convolution fusion | flops 809893888 | bytes 1761281 | tf_op jit(solution)/shard_map/while/body/eval_jaxpr/cgr,skgr->csk/dot_general | solution.py:49
  117.6 3.2 %fusion.57 = f32[512,12,32]{0,2,1:T(8,128)} fusion(s32[8,256]{1,0:T(8,128)S(1)} %get-tuple-element.188, f32[512,12,32]{0,2,1:T(8,128)} %get-tuple-element.199, bf16[32,8,256]{2,0,1:T(8,128)(2,1)S(1)} %dynamic-slice_bitcast_fusion.2, bf16[12,8,256]{2,1,0:T(8,128)(2,1)S(1)} %fusion.56, pred[]{:T(512)S(6)} %compare.13), kind=kOutput, calls=%fused_computation.6.clone.1 | convolution fusion | flops 809893888 | bytes 1761281 | tf_op jit(solution)/shard_map/while/body/eval_jaxpr/cgr,skgr->csk/dot_general | solution.py:49
  129.1 6.0 %collective-permute-done.1 = bf16[17,1,256]{2,1,0:T(2,128)(2,1)S(1)} collective-permute-done((bf16[17,1,256]{2,1,0:T(2,128)(2,1)S(1)}, bf16[17,1,256]{2,1,0:T(2,128)(2,1)S(1)}, u32[]{:S(2)}, u32[]{:S(2)}) %collective-permute-start.1) | collective-permute-done | bytes 8736 | tf_op jit(solution)/shard_map/ppermute | solution.py:23
  136.7 5.1 %collective-permute-start.3 = (bf16[8,1,256]{2,1,0:T(2,128)(2,1)S(1)}, bf16[8,1,256]{2,1,0:T(2,128)(2,1)S(1)}, u32[]{:S(2)}, u32[]{:S(2)}) collective-permute-start(bf16[8,1,256]{2,1,0:T(2,128)(2,1)S(1)} %get-tuple-element.151), channel_id=1, source_target_pairs={{4,0},{8,4},{12,8},{16,12},{20,16},{24,20},{28,24},{32,28},{36,32}... | collective-permute-start | bytes 12296 | tf_op jit(solution)/shard_map/ppermute | solution.py:34
  143.1 4.2 %collective-permute-start.4 = (bf16[1,18,256]{2,1,0:T(8,128)(2,1)S(1)}, bf16[1,18,256]{2,1,0:T(8,128)(2,1)S(1)}, u32[]{:S(2)}, u32[]{:S(2)}) collective-permute-start(bf16[1,18,256]{2,1,0:T(8,128)(2,1)S(1)} %get-tuple-element.148), channel_id=1, source_target_pairs={{0,1},{1,2},{2,3},{4,5},{5,6},{6,7},{8,9},{9,10},{10,11},{12,13},{... | collective-permute-start | bytes 27656 | tf_op jit(solution)/shard_map/ppermute | solution.py:33
  148.7 4.2 %collective-permute-done.5 = bf16[1,18,256]{2,1,0:T(8,128)(2,1)S(1)} collective-permute-done((bf16[1,18,256]{2,1,0:T(8,128)(2,1)S(1)}, bf16[1,18,256]{2,1,0:T(8,128)(2,1)S(1)}, u32[]{:S(2)}, u32[]{:S(2)}) %collective-permute-start.5) | collective-permute-done | bytes 9248 | tf_op jit(solution)/shard_map/ppermute | solution.py:34
  (115 shorter events, 36.2 us)
Async XLA Ops:
  0.0 136.2 %copy-start = (bf16[9,256,256]{2,1,0:T(8,128)(2,1)S(1)}, bf16[9,256,256]{2,1,0:T(8,128)(2,1)}, u32[]{:S(2)}) copy-start(bf16[9,256,256]{2,1,0:T(8,128)(2,1)} %param.20) | copy-start | bytes 3538948
  1.9 20.5 %all-to-all-start = ((s32[128,1,256]{2,1,0:T(1,128)}), s32[128,1,256]{2,1,0:T(1,128)S(1)}, u32[]{:S(2)}, u32[]{:S(2)}) async-start(s32[128,1,256]{2,1,0:T(1,128)} %all_to_all.11), calls=%async_computation | async-start | bytes 262144 | tf_op jit(solution)/shard_map/all_to_all | solution.py:85
  22.5 36.8 %all-to-all-start.1 = ((bf16[128,32,256]{2,1,0:T(8,128)(2,1)}), bf16[128,32,256]{2,1,0:T(8,128)(2,1)S(1)}, u32[]{:S(2)}, u32[]{:S(2)}) async-start(bf16[128,32,256]{2,1,0:T(8,128)(2,1)} %pad_maximum_fusion), calls=%async_computation.1 | async-start | bytes 4194304 | tf_op jit(solution)/shard_map/all_to_all | solution.py:84
  120.8 3.3 %copy-start.4 = (bf16[384,256]{1,0:T(8,128)(2,1)S(1)}, bf16[384,256]{1,0:T(8,128)(2,1)}, u32[]{:S(2)}) copy-start(bf16[384,256]{1,0:T(8,128)(2,1)} %param.18) | copy-start | bytes 589828
  120.8 3.3 %copy-start.5 = (f32[256]{0:T(256)S(1)}, f32[256]{0:T(256)}, u32[]{:S(2)}) copy-start(f32[256]{0:T(256)} %param.19) | copy-start | bytes 3076
  124.5 11.7 %copy-start.2 = (f32[256]{0:T(256)S(1)}, f32[256]{0:T(256)}, u32[]{:S(2)}) copy-start(f32[256]{0:T(256)} %param.21) | copy-start | bytes 3076
  124.5 4.0 %collective-permute-start = (bf16[1,32,256]{2,1,0:T(8,128)(2,1)S(1)}, bf16[1,32,256]{2,1,0:T(8,128)(2,1)S(1)}, u32[]{:S(2)}, u32[]{:S(2)}) collective-permute-start(bf16[1,32,256]{2,1,0:T(8,128)(2,1)S(1)} %slice_bitcast_fusion), channel_id=1, source_target_pairs={{0,1},{1,2},{2,3},{4,5},{5,6},{6,7},{8,9},{9,10},{10,11},{12,13},{... | collective-permute-start | bytes 49160 | tf_op jit(solution)/shard_map/ppermute | solution.py:17
  128.5 6.6 %collective-permute-start.1 = (bf16[17,1,256]{2,1,0:T(2,128)(2,1)S(1)}, bf16[17,1,256]{2,1,0:T(2,128)(2,1)S(1)}, u32[]{:S(2)}, u32[]{:S(2)}) collective-permute-start(bf16[17,1,256]{2,1,0:T(2,128)(2,1)S(1)} %fusion.41), channel_id=1, source_target_pairs={{0,4},{4,8},{8,12},{12,16},{16,20},{20,24},{24,28},{28,32},{32,36}... | collective-permute-start | bytes 26120 | tf_op jit(solution)/shard_map/ppermute | solution.py:23
  129.1 19.5 %copy-start.1 = (f32[9,256]{1,0:T(8,128)S(1)}, f32[9,256]{1,0:T(8,128)}, u32[]{:S(2)}) copy-start(f32[9,256]{1,0:T(8,128)} %param.22) | copy-start | bytes 27652
  136.0 17.4 %copy-start.3 = (f32[256]{0:T(256)S(1)}, f32[256]{0:T(256)}, u32[]{:S(2)}) copy-start(f32[256]{0:T(256)} %param.23) | copy-start | bytes 3076
  136.6 6.5 %collective-permute-start.2 = (bf16[8,1,256]{2,1,0:T(2,128)(2,1)S(1)}, bf16[8,1,256]{2,1,0:T(2,128)(2,1)S(1)}, u32[]{:S(2)}, u32[]{:S(2)}) collective-permute-start(bf16[8,1,256]{2,1,0:T(2,128)(2,1)S(1)} %get-tuple-element.150), channel_id=1, source_target_pairs={{0,4},{4,8},{8,12},{12,16},{16,20},{20,24},{24,28},{28,32},{32,36}... | collective-permute-start | bytes 12296 | tf_op jit(solution)/shard_map/ppermute | solution.py:33
  136.7 6.4 %collective-permute-start.3 = (bf16[8,1,256]{2,1,0:T(2,128)(2,1)S(1)}, bf16[8,1,256]{2,1,0:T(2,128)(2,1)S(1)}, u32[]{:S(2)}, u32[]{:S(2)}) collective-permute-start(bf16[8,1,256]{2,1,0:T(2,128)(2,1)S(1)} %get-tuple-element.151), channel_id=1, source_target_pairs={{4,0},{8,4},{12,8},{16,12},{20,16},{24,20},{28,24},{32,28},{36,32}... | collective-permute-start | bytes 12296 | tf_op jit(solution)/shard_map/ppermute | solution.py:34
  143.1 5.6 %collective-permute-start.4 = (bf16[1,18,256]{2,1,0:T(8,128)(2,1)S(1)}, bf16[1,18,256]{2,1,0:T(8,128)(2,1)S(1)}, u32[]{:S(2)}, u32[]{:S(2)}) collective-permute-start(bf16[1,18,256]{2,1,0:T(8,128)(2,1)S(1)} %get-tuple-element.148), channel_id=1, source_target_pairs={{0,1},{1,2},{2,3},{4,5},{5,6},{6,7},{8,9},{9,10},{10,11},{12,13},{... | collective-permute-start | bytes 27656 | tf_op jit(solution)/shard_map/ppermute | solution.py:33
  147.3 5.6 %collective-permute-start.5 = (bf16[1,18,256]{2,1,0:T(8,128)(2,1)S(1)}, bf16[1,18,256]{2,1,0:T(8,128)(2,1)S(1)}, u32[]{:S(2)}, u32[]{:S(2)}) collective-permute-start(bf16[1,18,256]{2,1,0:T(8,128)(2,1)S(1)} %get-tuple-element.149), channel_id=1, source_target_pairs={{1,0},{2,1},{3,2},{5,4},{6,5},{7,6},{9,8},{10,9},{11,10},{13,12},{... | collective-permute-start | bytes 27656 | tf_op jit(solution)/shard_map/ppermute | solution.py:34
where the time goes:
time: 156 us; the launch traced here: 154 us
  matrix products  50.3 us (32%)
  waiting for transfers between devices  44.4 us (28%)
  starting transfers between devices  31 us (20%)
  other arithmetic  22.6 us (14%)
  local copies, waits for them, and re-layouts  5.18 us (3%)
    dot_general x16, matrix products, spread_block(): jnp.einsum('cgr,skgr->csk', cell_hot, spread, preferred_element_type=jnp....  49.5 us
    all_to_all x1, waiting for transfers between devices, on_device(): lax.all_to_all(packed, ('lon', 'lat'), split_axis=0, concat_axis=0, tiled...  29.5 us
    select_n x16, other arithmetic, spread_block(): slot_of = codes // CELLS  11.3 us
    all_to_all x1, starting transfers between devices, on_device(): lax.all_to_all(codes, ('lon', 'lat'), split_axis=0, concat_axis=0, tiled=...  11.1 us
    all_to_all x1, starting transfers between devices, on_device(): lax.all_to_all(packed, ('lon', 'lat'), split_axis=0, concat_axis=0, tiled...  6.67 us
    ppermute x2, starting transfers between devices, with_halo(): after = lax.ppermute(leading, axis, down)  6.34 us
    ppermute x1, waiting for transfers between devices, shifted_2(): return lax.ppermute(value, axis, pairs)  5.97 us
    another operation x3, other arithmetic  5.66 us
  transfers between devices with their start and end apart: 8, of which 7 were waited for; matrix products, arithmetic and copies ran while one was open for 6% of the time, Pallas kernels for 0%

commit v1 on v0

v1 whole, which is shorter than its diff:
```python
import functools

import jax
import jax.numpy as jnp
import numpy as np
from jax import lax
from jax.experimental import pallas as pl
from jax.experimental.pallas import tpu as pltpu
from jax.sharding import PartitionSpec as P

MESH = pl.DeviceIdType.MESH
D = 256
OBS_VARS = 31
WIDTH = 32
SLOTS = 12
TLAT = 16
TLON = 32
CELLS = 512
GROUP = 8
BF16 = jnp.bfloat16
F32 = jnp.float32


def cell_number(row, col):
    return ((row % 2) * 2 + col % 2) * 128 + (row // 2) * 16 + col // 2


def strip_table():
    table = np.zeros((80, CELLS), np.float32)
    for row in range(TLAT):
        for i in range(3):
            table[row * 3 + i, cell_number(row, TLON - 3 + i)] = 1
        for i in range(2):
            table[48 + row * 2 + i, cell_number(row, i)] = 1
    return table


def rim_table():
    table = np.zeros((4, 12, 16, 256), np.float32)
    for plane in range(4):
        row_odd, col_odd = divmod(plane, 2)
        for p in range(-2, 9):
            row = 2 * p + row_odd
            if row < -3 or row > 17:
                continue
            for q in (-2, -1, 16):
                if q == -2 and not col_odd:
                    continue
                if q < 0:
                    i = 2 * q + col_odd + 3
                    if row < 0:
                        source = 80 + (row + 16) * 3 + i - 32
                    elif row < 16:
                        source = row * 3 + i
                    else:
                        source = 112 + (row - 16) * 3 + i
                    table[plane, p + 2, 16 + q, source] = 1
                else:
                    i = col_odd
                    if row < 0:
                        source = 96 + (row + 16) * 2 + i - 16
                    elif row < 16:
                        source = 48 + row * 2 + i
                    else:
                        source = 128 + (row - 16) * 2 + i
                    table[plane, p + 3, 0, source] = 1
    return table.reshape(4 * 12 * 16, 256)


def gelu(x):
    return 0.5 * x * (1.0 + jnp.tanh(0.7978845608028654 * (x + 0.044715 * (x * x * x))))


def far_first(dims):
    nx, nz, nc, ny = dims
    offsets = [
        (dx, dz, dc, dy)
        for dx in range(nx)
        for dz in range(nz)
        for dc in range(nc)
        for dy in range(ny)
        if dx or dz or dc or dy
    ]
    scrambled = sorted(offsets, key=lambda o: (o[0] * 37 + o[1] * 59 + o[2] * 83 + o[3] * 101) % 127)

    def length(o):
        return min(o[0], nx - o[0]) + min(o[1], nz - o[1]) + min(o[3], ny - o[3])

    return sorted(scrambled, key=lambda o: -length(o))


def kernel(
    dims,
    values_ref,
    offset_ref,
    cell_ref,
    slot_ref,
    count_ref,
    embed_weight_hbm,
    embed_bias_ref,
    stride_weight_hbm,
    stride_bias_ref,
    depth_weight_ref,
    gain_ref,
    strip_hbm,
    rim_hbm,
    out_ref,
    aux_ref,
    recv_ref,
    recv_aux_ref,
    spread_ref,
    hot_ref,
    total_ref,
    embed_weight_ref,
    stride_weight_ref,
    strip_ref,
    rim_ref,
    tile_ref,
    strips_ref,
    halo_ref,
    framed_ref,
    send_sem,
    recv_sem,
    local_sem,
    halo_send_sem,
    halo_recv_sem,
):
    nx, nz, nc, ny = dims
    lons = nx * nz * nc
    tiles = lons * ny
    groups = tiles // GROUP
    lon, lat = lax.axis_index("lon"), lax.axis_index("lat")
    core = lon % nc
    z = (lon // nc) % nz
    x = lon // (nc * nz)

    def wrapped(value, size):
        return jnp.where(value >= size, value - size, value)

    at_x = [wrapped(x + i, nx) * (nz * nc) for i in range(nx)]
    at_z = [wrapped(z + i, nz) * nc for i in range(nz)]
    at_core = [wrapped(core + i, nc) for i in range(nc)]
    at_y = [wrapped(lat + i, ny) for i in range(ny)]
    order = far_first(dims)
    partners = [(at_x[o[0]] + at_z[o[1]] + at_core[o[2]], at_y[o[3]]) for o in order]

    barrier = pltpu.get_barrier_semaphore()
    for partner in partners:
        pl.semaphore_signal(barrier, inc=1, device_id=partner, device_id_type=MESH)

    halo_ref[...] = jnp.zeros_like(halo_ref)
    me = lon * ny + lat
    own = pltpu.make_async_copy(values_ref.at[me], recv_ref.at[0], local_sem.at[0])
    own.start()
    loads = [
        pltpu.make_async_copy(source, target, local_sem.at[i])
        for i, (source, target) in enumerate(
            (
                (embed_weight_hbm, embed_weight_ref),
                (stride_weight_hbm, stride_weight_ref),
                (strip_hbm, strip_ref),
                (rim_hbm, rim_ref),
            ),
            1,
        )
    ]

    lane = lax.broadcasted_iota(jnp.int32, (tiles, tiles), 1)
    line = lax.broadcasted_iota(jnp.int32, (tiles, tiles), 0)
    count = jnp.sum(
        jnp.where(lane == line, count_ref[...].astype(F32), 0.0), axis=1, keepdims=True
    )
    position = lax.broadcasted_iota(jnp.int32, cell_ref.shape, 1).astype(F32)
    off_y, off_x = offset_ref[:, 0, :], offset_ref[:, 1, :]
    weight = jnp.where(position < count, jnp.exp(-2.0 * (off_y * off_y + off_x * off_x)), 0.0)
    cell = cell_ref[...]
    row, col = cell >> 5, cell & 31
    code = (
        slot_ref[...] * CELLS
        + (((row & 1) * 2 + (col & 1)) * 128 + (row >> 1) * 16 + (col >> 1))
    ).astype(F32)
    aux_ref[:, 0, :] = weight
    aux_ref[:, 1, :] = code

    pl.semaphore_wait(barrier, tiles - 1)

    def send_values(source, target, sem, partner):
        return pltpu.make_async_remote_copy(
            values_ref.at[source],
            recv_ref.at[target],
            send_sem.at[0],
            recv_sem.at[sem],
            device_id=partner,
            device_id_type=MESH,
        )

    def send_aux(source, target, sem, partner):
        return pltpu.make_async_remote_copy(
            aux_ref.at[source],
            recv_aux_ref.at[target],
            send_sem.at[1],
            recv_sem.at[sem + groups],
            device_id=partner,
            device_id_type=MESH,
        )

    for i, partner in enumerate(partners, 1):
        to = partner[0] * ny + partner[1]
        send_aux(to, i, i // GROUP, partner).start()
        send_values(to, i, i // GROUP, partner).start()

    for load in loads:
        load.start()
    own_aux = pltpu.make_async_copy(aux_ref.at[me], recv_aux_ref.at[0], local_sem.at[5])
    own_aux.start()
    total_ref[...] = jnp.zeros_like(total_ref)
    own.wait()
    own_aux.wait()

    cells = lax.broadcasted_iota(jnp.int32, (CELLS, 256), 0).astype(F32)

    def scatter(group):
        def build(i, carry):
            at = group * GROUP + i
            w = recv_aux_ref[at, 0:1, :]
            code = recv_aux_ref[at, 1:2, :]
            slot = jnp.floor(code * (1.0 / CELLS))
            cell = code - slot * CELLS
            scaled = recv_ref[at].astype(F32) * w
            packed = jnp.concatenate([scaled, w], axis=0)
            lanes = pl.ds(pl.multiple_of(i * 256, 256), 256)
            for s in range(SLOTS):
                spread_ref[s * WIDTH : (s + 1) * WIDTH, lanes] = jnp.where(
                    slot == s, packed, 0.0
                ).astype(BF16)
            hot_ref[:, lanes] = jnp.where(cells == cell, 1.0, 0.0).astype(BF16)
            return carry

        lax.fori_loop(0, GROUP, build, 0)
        total_ref[...] += lax.dot_general(
            spread_ref[...],
            hot_ref[...],
            (((1,), (1,)), ((), ())),
            preferred_element_type=F32,
        )

    def arrive(group, first, size):
        send_aux(pl.ds(first, size), pl.ds(first, size), group, partners[0]).wait_recv()
        send_values(pl.ds(first, size), pl.ds(first, size), group, partners[0]).wait_recv()

    def group_step(group, carry):
        @pl.when(group == 0)
        def _():
            arrive(0, 1, GROUP - 1)

        @pl.when(group > 0)
        def _():
            arrive(group, group * GROUP, GROUP)

        scatter(group)
        return carry

    lax.fori_loop(0, groups, group_step, 0)

    for load in loads:
        load.wait()

    total = total_ref[...].reshape(SLOTS, WIDTH, CELLS)
    density = total[:, WIDTH - 1 :, :]
    variable = lax.broadcasted_iota(jnp.int32, (SLOTS, WIDTH, CELLS), 1)
    gridded = jnp.where(variable == WIDTH - 1, total, total / (1.0 + density))
    gridded = gridded.reshape(SLOTS * WIDTH, CELLS).astype(BF16)
    projected = lax.dot_general(
        gridded, embed_weight_ref[...], (((0,), (0,)), ((), ())), preferred_element_type=F32
    )
    embedded = gelu(projected + embed_bias_ref[...]).astype(BF16)
    tile_ref[...] = embedded.reshape(4, 8, 16, D)
    strips_ref[...] = jnp.dot(strip_ref[...], embedded, preferred_element_type=F32).astype(BF16)

    right, left = wrapped(lon + 1, lons), wrapped(lon + lons - 1, lons)
    below, above = wrapped(lat + 1, ny), wrapped(lat + ny - 1, ny)

    def rows(i, source, target, partner):
        return pltpu.make_async_remote_copy(
            source,
            target,
            halo_send_sem.at[i],
            halo_recv_sem.at[i],
            device_id=partner,
            device_id_type=MESH,
        )

    exchange = [
        rows(0, tile_ref.at[2:4, 6:8], framed_ref.at[2:4, 0:2, 1], (lon, below)),
        rows(1, tile_ref.at[0:2, 7:8], framed_ref.at[0:2, 1:2, 1], (lon, below)),
        rows(2, tile_ref.at[0:4, 0:1], framed_ref.at[0:4, 10:11, 1], (lon, above)),
        rows(3, strips_ref.at[0:48], halo_ref.at[0:48], (right, lat)),
        rows(4, strips_ref.at[48:80], halo_ref.at[48:80], (left, lat)),
        rows(5, strips_ref.at[32:48], halo_ref.at[80:96], (right, below)),
        rows(6, strips_ref.at[64:80], halo_ref.at[96:112], (left, below)),
        rows(7, strips_ref.at[0:16], halo_ref.at[112:128], (right, above)),
        rows(8, strips_ref.at[48:64], halo_ref.at[128:144], (left, above)),
    ]
    for copy in reversed(exchange):
        copy.start()
    framed_ref[:, 2:10, 1] = embedded.reshape(4, 8, 16, D)
    for copy in exchange:
        copy.wait_recv()

    @pl.when(lat == 0)
    def _():
        halo_ref[80:112] = jnp.zeros((32, D), BF16)
        framed_ref[2:4, 1, 1] = jnp.zeros((2, 16, D), BF16)

    rim = jnp.dot(rim_ref[...], halo_ref[...], preferred_element_type=F32).astype(BF16)
    framed_ref[:, :, 0] = rim.reshape(4, 12, 16, D)

    planes = [framed_ref[i].reshape(384, D) for i in range(4)]
    span = 336

    def tap(a, c):
        plane = planes[(0 if a == 1 else 2) + (0 if c == 1 else 1)]
        base = 0 if a == 0 else 32
        return jnp.dot(
            plane[base : base + span], stride_weight_ref[3 * a + c], preferred_element_type=F32
        )

    before = tap(0, 0) + tap(1, 0) + tap(2, 0)
    here = tap(0, 1) + tap(1, 1) + tap(2, 1) + tap(0, 2) + tap(1, 2) + tap(2, 2)
    strided = pltpu.roll(before, 1, 0) + here + stride_bias_ref[...]
    coarse = gelu(strided).astype(BF16).astype(F32)
    at = lax.broadcasted_iota(jnp.int32, (span, D), 0)
    low = jnp.where(lat == 0, 40, 0)
    high = jnp.where(lat == ny - 1, 296, span)
    coarse = jnp.where((at >= low) & (at < high), coarse, 0.0)

    reach = 272

    def column(c):
        total = coarse[0:reach] * depth_weight_ref[c : c + 1]
        for a in (1, 2):
            total = total + coarse[32 * a : 32 * a + reach] * depth_weight_ref[3 * a + c : 3 * a + c + 1]
        return total

    mixed = (
        coarse[32 : 32 + reach]
        + column(1)
        + pltpu.roll(column(0), 1, 0)
        + pltpu.roll(column(2), reach - 1, 0)
    )
    mixed = mixed[:256].reshape(8, 2, 16, D)[:, 1]
    centre = mixed - jnp.mean(mixed, axis=-1, keepdims=True)
    variance = jnp.mean(centre * centre, axis=-1, keepdims=True)
    out_ref[...] = (centre * lax.rsqrt(variance + 1e-05) * gain_ref[...][None]).astype(BF16)

    for copy in exchange:
        copy.wait_send()
    send_aux(pl.ds(1, tiles - 1), pl.ds(1, tiles - 1), 0, partners[0]).wait_send()
    send_values(pl.ds(1, tiles - 1), pl.ds(1, tiles - 1), 0, partners[0]).wait_send()


def physical(lons, lats):
    nc = 2
    nz = 4 if lons % 8 == 0 else 2
    return (lons // (nc * nz), nz, nc, lats)


def solution(mesh):
    dims = physical(mesh.shape["lon"], mesh.shape["lat"])
    tiles = mesh.shape["lon"] * mesh.shape["lat"]
    groups = tiles // GROUP
    vmem = pl.BlockSpec(memory_space=pltpu.VMEM)
    anywhere = pl.BlockSpec(memory_space=pl.ANY)
    strips, rims = strip_table(), rim_table()

    def on_device(
        obs_values,
        obs_offset,
        obs_cell,
        obs_slot,
        obs_count,
        embed_weight,
        embed_bias,
        stride_weight,
        stride_bias,
        depth_weight,
        norm_gain,
    ):
        return pl.pallas_call(
            functools.partial(kernel, dims),
            out_shape=jax.ShapeDtypeStruct((TLAT // 2, TLON // 2, D), BF16),
            in_specs=[
                anywhere,
                vmem,
                vmem,
                vmem,
                vmem,
                anywhere,
                vmem,
                anywhere,
                vmem,
                vmem,
                vmem,
                anywhere,
                anywhere,
            ],
            out_specs=vmem,
            scratch_shapes=[
                pltpu.VMEM((tiles, 2, 256), F32),
                pltpu.VMEM((tiles, OBS_VARS, 256), BF16),
                pltpu.VMEM((tiles, 2, 256), F32),
                pltpu.VMEM((SLOTS * WIDTH, GROUP * 256), BF16),
                pltpu.VMEM((CELLS, GROUP * 256), BF16),
                pltpu.VMEM((SLOTS * WIDTH, CELLS), F32),
                pltpu.VMEM((SLOTS * WIDTH, D), BF16),
                pltpu.VMEM((9, D, D), BF16),
                pltpu.VMEM((80, CELLS), BF16),
                pltpu.VMEM((768, 256), BF16),
                pltpu.VMEM((4, 8, 16, D), BF16),
                pltpu.VMEM((80, D), BF16),
                pltpu.VMEM((256, D), BF16),
                pltpu.VMEM((4, 12, 2, 16, D), BF16),
                pltpu.SemaphoreType.DMA((2,)),
                pltpu.SemaphoreType.DMA((2 * groups,)),
                pltpu.SemaphoreType.DMA((6,)),
                pltpu.SemaphoreType.DMA((9,)),
                pltpu.SemaphoreType.DMA((9,)),
            ],
            compiler_params=pltpu.CompilerParams(
                collective_id=0, has_side_effects=True, vmem_limit_bytes=60 << 20
            ),
        )(
            obs_values,
            obs_offset,
            obs_cell,
            obs_slot,
            obs_count,
            embed_weight,
            embed_bias[None],
            stride_weight,
            stride_bias[None],
            depth_weight,
            norm_gain[None],
            jnp.asarray(strips, BF16),
            jnp.asarray(rims, BF16),
        )

    placed = (
        P(("lon", "lat"), None, None),
        P(("lon", "lat"), None, None),
        P(("lon", "lat"), None),
        P(("lon", "lat"), None),
        P(("lon", "lat"), None),
        P(),
        P(),
        P(),
        P(),
        P(),
        P(),
    )
    return jax.shard_map(
        on_device, mesh=mesh, in_specs=placed, out_specs=P("lat", "lon", None), check_vma=False
    )
```

time: 156 us -> 62.9 us (0.40)
  Pallas kernels: 0 us -> 56.9 us
  matrix products: 50.3 us -> 0 us
  waiting for transfers between devices: 44.4 us -> 0 us
  starting transfers between devices: 31 us -> 0 us
  other arithmetic: 22.6 us -> 0 us
    pallas_call x0 -> x1, Pallas kernels: none -> 56.9 us  [on_device(): pl.pallas_call(functools.partial(kernel, dims), out_shape=jax.ShapeDtypeS...]
    dot_general x18 -> x0, matrix products: 50.3 us -> none  [the longest x16 49.5 us: spread_block(): jnp.einsum('cgr,skgr->csk', cell_hot, spread, preferred_element_type=jnp....]
    all_to_all x2 -> x0, waiting for transfers between devices: 32.6 us -> none  [the longest x1 29.5 us: on_device(): lax.all_to_all(packed, ('lon', 'lat'), split_axis=0, concat_axis=0, tiled...]
    all_to_all x2 -> x0, starting transfers between devices: 17.8 us -> none  [the longest x1 11.1 us: on_device(): lax.all_to_all(codes, ('lon', 'lat'), split_axis=0, concat_axis=0, tiled=...]
    ppermute x6 -> x0, starting transfers between devices: 13.2 us -> none  [the longest x2 6.34 us: with_halo(): after = lax.ppermute(leading, axis, down)]
    select_n x17 -> x0, other arithmetic: 12.4 us -> none  [the longest x16 11.3 us: spread_block(): slot_of = codes // CELLS]
    ppermute x6 -> x0, waiting for transfers between devices: 11.8 us -> none  [the longest x1 5.97 us: shifted_2(): return lax.ppermute(value, axis, pairs)]
    another operation x3 -> x0, other arithmetic: 5.66 us -> none
  transfers between devices with their start and end apart: 8 -> 0, of which waited for: 7 -> 0; matrix products, arithmetic and copies ran while one was open for 6% -> 0% of each run, Pallas kernels for 0% -> 0%
where the time goes in v1:
time: 62.9 us; the launch traced here: 62.5 us
  Pallas kernels  56.9 us (90%)
  local copies, waits for them, and re-layouts  5.53 us (9%)
    pallas_call x1, Pallas kernels, on_device(): pl.pallas_call(functools.partial(kernel, dims), out_shape=jax.ShapeDtypeS...  56.9 us
    unnamed x2, local copies, waits for them, and re-layouts  5.53 us

profile of v1, /device:TPU:0, one launch (start us, length us, event | category | flops | bytes accessed | tf_op | source)
XLA Modules:
  0.0 62.5 jit_solution(9575507368897589611)
XLA Ops:
  0.0 4.1 %copy.14.values_ref = bf16[128,31,256]{2,1,0:T(8,128)(2,1)} copy(bf16[128,31,256]{2,0,1:T(8,128)(2,1)} %param.13) | data formatting | bytes 4063232 | tf_op args[0]
  4.1 56.9 %shard_map.127 = bf16[8,16,256]{2,1,0:T(8,128)(2,1)} custom-call(bf16[128,31,256]{2,1,0:T(8,128)(2,1)} %copy.14.values_ref, f32[128,2,256]{2,1,0:T(2,128)} %offset_ref.1, s32[128,256]{1,0:T(8,128)} %cell_ref.1, s32[128,256]{1,0:T(8,128)} %slot_ref.1, s32[1,128]{1,0:T(1,128)} %count_ref.1, bf16[384,256]{1,0:T(8,128)(2,1)} %embed_weight_hbm.1, ...), custom_call_target="tpu_custom_call" | custom-call | tf_op jit(solution)/shard_map/pallas_call | solution.py:389
  61.0 1.5 %copy.16 = bf16[8,16,256]{2,1,0:T(8,128)(2,1)} copy(bf16[8,16,256]{2,1,0:T(8,128)(2,1)} %shard_map.127) | data formatting | bytes 131072

commit v2 on v1

--- a/solution.py
+++ b/solution.py
@@ -19,6 +19,7 @@
 GROUP = 8
 BF16 = jnp.bfloat16
 F32 = jnp.float32
+PITCH = 136
 
 
 def cell_number(row, col):
@@ -105,9 +106,12 @@
     strip_hbm,
     rim_hbm,
     out_ref,
-    aux_ref,
+    raw_ref,
+    wide_ref,
+    packed_ref,
+    code_ref,
     recv_ref,
-    recv_aux_ref,
+    recv_code_ref,
     spread_ref,
     hot_ref,
     total_ref,
@@ -144,14 +148,21 @@
     order = far_first(dims)
     partners = [(at_x[o[0]] + at_z[o[1]] + at_core[o[2]], at_y[o[3]]) for o in order]
 
+    chunks = ((0, 8), (8, 16), (16, 24), (24, 31))
+    raws = [
+        pltpu.make_async_copy(
+            values_ref.at[low:high], raw_ref.at[low:high], local_sem.at[5 + i]
+        )
+        for i, (low, high) in enumerate(chunks)
+    ]
+    for raw in raws:
+        raw.start()
     barrier = pltpu.get_barrier_semaphore()
     for partner in partners:
         pl.semaphore_signal(barrier, inc=1, device_id=partner, device_id_type=MESH)
 
     halo_ref[...] = jnp.zeros_like(halo_ref)
     me = lon * ny + lat
-    own = pltpu.make_async_copy(values_ref.at[me], recv_ref.at[0], local_sem.at[0])
-    own.start()
     loads = [
         pltpu.make_async_copy(source, target, local_sem.at[i])
         for i, (source, target) in enumerate(
@@ -179,14 +190,29 @@
         slot_ref[...] * CELLS
         + (((row & 1) * 2 + (col & 1)) * 128 + (row >> 1) * 16 + (col >> 1))
     ).astype(F32)
-    aux_ref[:, 0, :] = weight
-    aux_ref[:, 1, :] = code
+    code_ref[:, 0, :] = code
+    def widen(k, row):
+        for h in range(2):
+            start = (h * WIDTH + k) * PITCH
+            wide_ref[start : start + tiles] = row[:, h * 128 : h * 128 + 128]
+
+    widen(31, weight)
+    for raw, (low, high) in zip(raws, chunks):
+        raw.wait()
+        for k in range(low, high):
+            widen(k, raw_ref[k].astype(F32) * weight)
+
+    def pack(target):
+        halves = [
+            wide_ref[pl.ds(target + h * WIDTH * PITCH, WIDTH, stride=PITCH), :] for h in range(2)
+        ]
+        return jnp.concatenate(halves, axis=1).astype(BF16)
 
     pl.semaphore_wait(barrier, tiles - 1)
 
     def send_values(source, target, sem, partner):
         return pltpu.make_async_remote_copy(
-            values_ref.at[source],
+            packed_ref.at[source],
             recv_ref.at[target],
             send_sem.at[0],
             recv_sem.at[sem],
@@ -194,10 +220,10 @@
             device_id_type=MESH,
         )
 
-    def send_aux(source, target, sem, partner):
+    def send_code(source, target, sem, partner):
         return pltpu.make_async_remote_copy(
-            aux_ref.at[source],
-            recv_aux_ref.at[target],
+            code_ref.at[source],
+            recv_code_ref.at[target],
             send_sem.at[1],
             recv_sem.at[sem + groups],
             device_id=partner,
@@ -206,37 +232,47 @@
 
     for i, partner in enumerate(partners, 1):
         to = partner[0] * ny + partner[1]
-        send_aux(to, i, i // GROUP, partner).start()
-        send_values(to, i, i // GROUP, partner).start()
+        packed_ref[i] = pack(to)
+        send_code(to, i, i // GROUP, partner).start()
+        send_values(i, i, i // GROUP, partner).start()
 
     for load in loads:
         load.start()
-    own_aux = pltpu.make_async_copy(aux_ref.at[me], recv_aux_ref.at[0], local_sem.at[5])
-    own_aux.start()
+    recv_ref[0] = pack(me)
+    recv_code_ref[0] = code_ref[me]
     total_ref[...] = jnp.zeros_like(total_ref)
-    own.wait()
-    own_aux.wait()
-
-    cells = lax.broadcasted_iota(jnp.int32, (CELLS, 256), 0).astype(F32)
+
+    line16 = lax.broadcasted_iota(jnp.int32, (16, 256), 0).astype(F32).astype(BF16)
 
     def scatter(group):
         def build(i, carry):
             at = group * GROUP + i
-            w = recv_aux_ref[at, 0:1, :]
-            code = recv_aux_ref[at, 1:2, :]
+            code = recv_code_ref[at]
             slot = jnp.floor(code * (1.0 / CELLS))
             cell = code - slot * CELLS
-            scaled = recv_ref[at].astype(F32) * w
-            packed = jnp.concatenate([scaled, w], axis=0)
+            half = jnp.where(cell >= 256, 1.0, 0.0)
+            low = cell - 256.0 * half
+            first = jnp.broadcast_to(jnp.where(half == 0.0, low, -1.0), (16, 256)).astype(BF16)
+            second = jnp.broadcast_to(jnp.where(half == 1.0, low, -1.0), (16, 256)).astype(BF16)
+            slot = jnp.broadcast_to(slot, (16, 256)).astype(BF16)
+            packed = recv_ref[at]
             lanes = pl.ds(pl.multiple_of(i * 256, 256), 256)
+            zero, one = jnp.zeros((16, 256), BF16), jnp.ones((16, 256), BF16)
             for s in range(SLOTS):
-                spread_ref[s * WIDTH : (s + 1) * WIDTH, lanes] = jnp.where(
-                    slot == s, packed, 0.0
-                ).astype(BF16)
-            hot_ref[:, lanes] = jnp.where(cells == cell, 1.0, 0.0).astype(BF16)
+                mine = slot == s
+                for h in range(2):
+                    spread_ref[s * WIDTH + h * 16 : s * WIDTH + h * 16 + 16, lanes] = jnp.where(
+                        mine, packed[h * 16 : h * 16 + 16], zero
+                    )
+            for h, wanted in enumerate((first, second)):
+                for r in range(16):
+                    at_row = h * 256 + r * 16
+                    hot_ref[at_row : at_row + 16, lanes] = jnp.where(
+                        wanted == line16 + (r * 16), one, zero
+                    )
             return carry
 
-        lax.fori_loop(0, GROUP, build, 0)
+        lax.fori_loop(0, GROUP, build, 0, unroll=True)
         total_ref[...] += lax.dot_general(
             spread_ref[...],
             hot_ref[...],
@@ -245,7 +281,7 @@
         )
 
     def arrive(group, first, size):
-        send_aux(pl.ds(first, size), pl.ds(first, size), group, partners[0]).wait_recv()
+        send_code(pl.ds(first, size), pl.ds(first, size), group, partners[0]).wait_recv()
         send_values(pl.ds(first, size), pl.ds(first, size), group, partners[0]).wait_recv()
 
     def group_step(group, carry):
@@ -355,7 +391,7 @@
 
     for copy in exchange:
         copy.wait_send()
-    send_aux(pl.ds(1, tiles - 1), pl.ds(1, tiles - 1), 0, partners[0]).wait_send()
+    send_code(pl.ds(1, tiles - 1), pl.ds(1, tiles - 1), 0, partners[0]).wait_send()
     send_values(pl.ds(1, tiles - 1), pl.ds(1, tiles - 1), 0, partners[0]).wait_send()
 
 
@@ -406,9 +442,12 @@
             ],
             out_specs=vmem,
             scratch_shapes=[
-                pltpu.VMEM((tiles, 2, 256), F32),
-                pltpu.VMEM((tiles, OBS_VARS, 256), BF16),
-                pltpu.VMEM((tiles, 2, 256), F32),
+                pltpu.VMEM((OBS_VARS, tiles, 256), BF16),
+                pltpu.VMEM((2 * WIDTH * PITCH, 128), F32),
+                pltpu.VMEM((tiles, WIDTH, 256), BF16),
+                pltpu.VMEM((tiles, 1, 256), F32),
+                pltpu.VMEM((tiles, WIDTH, 256), BF16),
+                pltpu.VMEM((tiles, 1, 256), F32),
                 pltpu.VMEM((SLOTS * WIDTH, GROUP * 256), BF16),
                 pltpu.VMEM((CELLS, GROUP * 256), BF16),
                 pltpu.VMEM((SLOTS * WIDTH, CELLS), F32),
@@ -422,7 +461,7 @@
                 pltpu.VMEM((4, 12, 2, 16, D), BF16),
                 pltpu.SemaphoreType.DMA((2,)),
                 pltpu.SemaphoreType.DMA((2 * groups,)),
-                pltpu.SemaphoreType.DMA((6,)),
+                pltpu.SemaphoreType.DMA((9,)),
                 pltpu.SemaphoreType.DMA((9,)),
                 pltpu.SemaphoreType.DMA((9,)),
             ],
@@ -430,7 +469,7 @@
                 collective_id=0, has_side_effects=True, vmem_limit_bytes=60 << 20
             ),
         )(
-            obs_values,
+            jnp.transpose(obs_values, (1, 0, 2)),
             obs_offset,
             obs_cell,
             obs_slot,

time: 62.9 us -> 51.6 us (0.82)
  Pallas kernels: 56.9 us -> 49.5 us
  local copies, waits for them, and re-layouts: 5.53 us -> 1.47 us
    pallas_call x1, Pallas kernels: 56.9 us -> 49.5 us  [on_device(): pl.pallas_call(functools.partial(kernel, dims), out_shape=jax.ShapeDtypeS...]
    unnamed x2 -> x1, local copies, waits for them, and re-layouts: 5.53 us -> 1.47 us
where the time goes in v2:
time: 51.6 us; the launch traced here: 51 us
  Pallas kernels  49.5 us (96%)
  local copies, waits for them, and re-layouts  1.47 us (3%)
    pallas_call x1, Pallas kernels, on_device(): pl.pallas_call(functools.partial(kernel, dims), out_shape=jax.ShapeDtypeS...  49.5 us
    unnamed x1, local copies, waits for them, and re-layouts  1.47 us

profile of v2, /device:TPU:0, one launch (start us, length us, event | category | flops | bytes accessed | tf_op | source)
XLA Modules:
  0.0 51.0 jit_solution(5159176783816796141)
XLA Ops:
  0.0 49.5 %shard_map.127 = bf16[8,16,256]{2,1,0:T(8,128)(2,1)} custom-call(bf16[31,128,256]{2,1,0:T(8,128)(2,1)} %bitcast.4, f32[128,2,256]{2,1,0:T(2,128)} %offset_ref.1, s32[128,256]{1,0:T(8,128)} %cell_ref.1, s32[128,256]{1,0:T(8,128)} %slot_ref.1, s32[1,128]{1,0:T(1,128)} %count_ref.1, bf16[384,256]{1,0:T(8,128)(2,1)} %embed_weight_hbm.1, f32[1,256]{1,0:T(1,128)} %bitcast.5, ...), custom_call_target="tpu_custom_call" | custom-call | tf_op jit(solution)/shard_map/pallas_call | solution.py:425
  49.5 1.5 %copy.15 = bf16[8,16,256]{2,1,0:T(8,128)(2,1)} copy(bf16[8,16,256]{2,1,0:T(8,128)(2,1)} %shard_map.127) | data formatting | bytes 131072

commit v3 on v2

--- a/solution.py
+++ b/solution.py
@@ -72,7 +72,7 @@
     return 0.5 * x * (1.0 + jnp.tanh(0.7978845608028654 * (x + 0.044715 * (x * x * x))))
 
 
-def far_first(dims):
+def scrambled(dims):
     nx, nz, nc, ny = dims
     offsets = [
         (dx, dz, dc, dy)
@@ -82,30 +82,33 @@
         for dy in range(ny)
         if dx or dz or dc or dy
     ]
-    scrambled = sorted(offsets, key=lambda o: (o[0] * 37 + o[1] * 59 + o[2] * 83 + o[3] * 101) % 127)
-
-    def length(o):
-        return min(o[0], nx - o[0]) + min(o[1], nz - o[1]) + min(o[3], ny - o[3])
-
-    return sorted(scrambled, key=lambda o: -length(o))
+    return sorted(offsets, key=lambda o: (o[0] * 37 + o[1] * 59 + o[2] * 83 + o[3] * 101) % 127)
 
 
 def kernel(
     dims,
     values_ref,
+    offset_hbm,
+    cell_hbm,
+    slot_hbm,
+    count_hbm,
+    embed_weight_hbm,
+    embed_bias_hbm,
+    stride_weight_hbm,
+    stride_bias_hbm,
+    depth_weight_hbm,
+    gain_hbm,
+    strip_hbm,
+    rim_hbm,
+    out_ref,
     offset_ref,
     cell_ref,
     slot_ref,
     count_ref,
-    embed_weight_hbm,
     embed_bias_ref,
-    stride_weight_hbm,
     stride_bias_ref,
     depth_weight_ref,
     gain_ref,
-    strip_hbm,
-    rim_hbm,
-    out_ref,
     raw_ref,
     wide_ref,
     packed_ref,
@@ -125,7 +128,9 @@
     framed_ref,
     send_sem,
     recv_sem,
-    local_sem,
+    first_sem,
+    raw_sem,
+    load_sem,
     halo_send_sem,
     halo_recv_sem,
 ):
@@ -145,36 +150,54 @@
     at_z = [wrapped(z + i, nz) * nc for i in range(nz)]
     at_core = [wrapped(core + i, nc) for i in range(nc)]
     at_y = [wrapped(lat + i, ny) for i in range(ny)]
-    order = far_first(dims)
+    order = scrambled(dims)
     partners = [(at_x[o[0]] + at_z[o[1]] + at_core[o[2]], at_y[o[3]]) for o in order]
 
+    barrier = pltpu.get_barrier_semaphore()
+    for partner in partners:
+        pl.semaphore_signal(barrier, inc=1, device_id=partner, device_id_type=MESH)
+
+    firsts = [
+        pltpu.make_async_copy(source, target, first_sem.at[i])
+        for i, (source, target) in enumerate(
+            (
+                (offset_hbm, offset_ref),
+                (count_hbm, count_ref),
+                (cell_hbm, cell_ref),
+                (slot_hbm, slot_ref),
+            )
+        )
+    ]
+    for first in firsts:
+        first.start()
     chunks = ((0, 8), (8, 16), (16, 24), (24, 31))
     raws = [
         pltpu.make_async_copy(
-            values_ref.at[low:high], raw_ref.at[low:high], local_sem.at[5 + i]
+            values_ref.at[low:high], raw_ref.at[low:high], raw_sem.at[i]
         )
         for i, (low, high) in enumerate(chunks)
     ]
     for raw in raws:
         raw.start()
-    barrier = pltpu.get_barrier_semaphore()
-    for partner in partners:
-        pl.semaphore_signal(barrier, inc=1, device_id=partner, device_id_type=MESH)
-
     halo_ref[...] = jnp.zeros_like(halo_ref)
     me = lon * ny + lat
     loads = [
-        pltpu.make_async_copy(source, target, local_sem.at[i])
+        pltpu.make_async_copy(source, target, load_sem.at[i])
         for i, (source, target) in enumerate(
             (
                 (embed_weight_hbm, embed_weight_ref),
                 (stride_weight_hbm, stride_weight_ref),
                 (strip_hbm, strip_ref),
                 (rim_hbm, rim_ref),
-            ),
-            1,
+                (embed_bias_hbm, embed_bias_ref),
+                (stride_bias_hbm, stride_bias_ref),
+                (depth_weight_hbm, depth_weight_ref),
+                (gain_hbm, gain_ref),
+            )
         )
     ]
+    for first in firsts:
+        first.wait()
 
     lane = lax.broadcasted_iota(jnp.int32, (tiles, tiles), 1)
     line = lax.broadcasted_iota(jnp.int32, (tiles, tiles), 0)
@@ -311,7 +334,6 @@
     )
     embedded = gelu(projected + embed_bias_ref[...]).astype(BF16)
     tile_ref[...] = embedded.reshape(4, 8, 16, D)
-    strips_ref[...] = jnp.dot(strip_ref[...], embedded, preferred_element_type=F32).astype(BF16)
 
     right, left = wrapped(lon + 1, lons), wrapped(lon + lons - 1, lons)
     below, above = wrapped(lat + 1, ny), wrapped(lat + ny - 1, ny)
@@ -337,7 +359,10 @@
         rows(7, strips_ref.at[0:16], halo_ref.at[112:128], (right, above)),
         rows(8, strips_ref.at[48:64], halo_ref.at[128:144], (left, above)),
     ]
-    for copy in reversed(exchange):
+    for copy in exchange[:3]:
+        copy.start()
+    strips_ref[...] = jnp.dot(strip_ref[...], embedded, preferred_element_type=F32).astype(BF16)
+    for copy in exchange[3:]:
         copy.start()
     framed_ref[:, 2:10, 1] = embedded.reshape(4, 8, 16, D)
     for copy in exchange:
@@ -425,23 +450,17 @@
         return pl.pallas_call(
             functools.partial(kernel, dims),
             out_shape=jax.ShapeDtypeStruct((TLAT // 2, TLON // 2, D), BF16),
-            in_specs=[
-                anywhere,
-                vmem,
-                vmem,
-                vmem,
-                vmem,
-                anywhere,
-                vmem,
-                anywhere,
-                vmem,
-                vmem,
-                vmem,
-                anywhere,
-                anywhere,
-            ],
+            in_specs=[anywhere] * 13,
             out_specs=vmem,
             scratch_shapes=[
+                pltpu.VMEM((tiles, 2, 256), F32),
+                pltpu.VMEM((tiles, 256), jnp.int32),
+                pltpu.VMEM((tiles, 256), jnp.int32),
+                pltpu.VMEM((1, tiles), jnp.int32),
+                pltpu.VMEM((1, D), F32),
+                pltpu.VMEM((1, D), F32),
+                pltpu.VMEM((9, D), F32),
+                pltpu.VMEM((1, D), F32),
                 pltpu.VMEM((OBS_VARS, tiles, 256), BF16),
                 pltpu.VMEM((2 * WIDTH * PITCH, 128), F32),
                 pltpu.VMEM((tiles, WIDTH, 256), BF16),
@@ -461,7 +480,9 @@
                 pltpu.VMEM((4, 12, 2, 16, D), BF16),
                 pltpu.SemaphoreType.DMA((2,)),
                 pltpu.SemaphoreType.DMA((2 * groups,)),
-                pltpu.SemaphoreType.DMA((9,)),
+                pltpu.SemaphoreType.DMA((4,)),
+                pltpu.SemaphoreType.DMA((4,)),
+                pltpu.SemaphoreType.DMA((8,)),
                 pltpu.SemaphoreType.DMA((9,)),
                 pltpu.SemaphoreType.DMA((9,)),
             ],

time: 51.6 us -> 48.8 us (0.946)
  Pallas kernels: 49.5 us -> 47.1 us
    pallas_call x1, Pallas kernels: 49.5 us -> 47.1 us  [on_device(): pl.pallas_call(functools.partial(kernel, dims), out_shape=jax.ShapeDtypeS...]
where the time goes in v3:
time: 48.8 us; the launch traced here: 48.6 us
  Pallas kernels  47.1 us (97%)
  local copies, waits for them, and re-layouts  1.47 us (3%)
    pallas_call x1, Pallas kernels, on_device(): pl.pallas_call(functools.partial(kernel, dims), out_shape=jax.ShapeDtypeS...  47.1 us
    unnamed x1, local copies, waits for them, and re-layouts  1.47 us

profile of v3, /device:TPU:0, one launch (start us, length us, event | category | flops | bytes accessed | tf_op | source)
XLA Modules:
  0.0 48.6 jit_solution(8068006913339493616)
XLA Ops:
  0.0 47.1 %shard_map.127 = bf16[8,16,256]{2,1,0:T(8,128)(2,1)} custom-call(bf16[31,128,256]{2,1,0:T(8,128)(2,1)} %bitcast.4, f32[128,2,256]{2,1,0:T(2,128)} %offset_hbm.1, s32[128,256]{1,0:T(8,128)} %cell_hbm.1, s32[128,256]{1,0:T(8,128)} %slot_hbm.1, s32[1,128]{1,0:T(1,128)} %count_hbm.1, bf16[384,256]{1,0:T(8,128)(2,1)} %embed_weight_hbm.1, f32[1,256]{1,0:T(1,128)} %bitcast.5, ...), custom_call_target="tpu_custom_call" | custom-call | tf_op jit(solution)/shard_map/pallas_call | solution.py:450
  47.1 1.5 %copy.15 = bf16[8,16,256]{2,1,0:T(8,128)(2,1)} copy(bf16[8,16,256]{2,1,0:T(8,128)(2,1)} %shard_map.127) | data formatting | bytes 131072

commit v4 on v3

--- a/solution.py
+++ b/solution.py
@@ -154,7 +154,11 @@
     partners = [(at_x[o[0]] + at_z[o[1]] + at_core[o[2]], at_y[o[3]]) for o in order]
 
     barrier = pltpu.get_barrier_semaphore()
-    for partner in partners:
+    def reach(o):
+        return min(o[0], nx - o[0]) + min(o[1], nz - o[1]) + min(o[3], ny - o[3])
+
+    greeted = sorted(range(len(order)), key=lambda i: -reach(order[i]))
+    for partner in [partners[i] for i in greeted]:
         pl.semaphore_signal(barrier, inc=1, device_id=partner, device_id_type=MESH)
 
     firsts = [

time: 48.8 us -> 48.1 us (0.986)
  Pallas kernels: 47.1 us -> 46.4 us
    pallas_call x1, Pallas kernels: 47.1 us -> 46.4 us  [on_device(): pl.pallas_call(functools.partial(kernel, dims), out_shape=jax.ShapeDtypeS...]
where the time goes in v4:
time: 48.1 us; the launch traced here: 47.9 us
  Pallas kernels  46.4 us (96%)
  local copies, waits for them, and re-layouts  1.47 us (3%)
    pallas_call x1, Pallas kernels, on_device(): pl.pallas_call(functools.partial(kernel, dims), out_shape=jax.ShapeDtypeS...  46.4 us
    unnamed x1, local copies, waits for them, and re-layouts  1.47 us

profile of v4, /device:TPU:0, one launch (start us, length us, event | category | flops | bytes accessed | tf_op | source)
XLA Modules:
  0.0 47.9 jit_solution(1976696904633629988)
XLA Ops:
  0.0 46.4 %shard_map.127 = bf16[8,16,256]{2,1,0:T(8,128)(2,1)} custom-call(bf16[31,128,256]{2,1,0:T(8,128)(2,1)} %bitcast.4, f32[128,2,256]{2,1,0:T(2,128)} %offset_hbm.1, s32[128,256]{1,0:T(8,128)} %cell_hbm.1, s32[128,256]{1,0:T(8,128)} %slot_hbm.1, s32[1,128]{1,0:T(1,128)} %count_hbm.1, bf16[384,256]{1,0:T(8,128)(2,1)} %embed_weight_hbm.1, f32[1,256]{1,0:T(1,128)} %bitcast.5, ...), custom_call_target="tpu_custom_call" | custom-call | tf_op jit(solution)/shard_map/pallas_call | solution.py:454
  46.5 1.5 %copy.15 = bf16[8,16,256]{2,1,0:T(8,128)(2,1)} copy(bf16[8,16,256]{2,1,0:T(8,128)(2,1)} %shard_map.127) | data formatting | bytes 131072

commit v5 on v4

--- a/solution.py
+++ b/solution.py
@@ -453,7 +453,7 @@
     ):
         return pl.pallas_call(
             functools.partial(kernel, dims),
-            out_shape=jax.ShapeDtypeStruct((TLAT // 2, TLON // 2, D), BF16),
+            out_shape=pltpu.VMEM((TLAT // 2, TLON // 2, D), BF16),
             in_specs=[anywhere] * 13,
             out_specs=vmem,
             scratch_shapes=[

time: 48.1 us -> 46.7 us (0.971)
  local copies, waits for them, and re-layouts: 1.47 us -> 0.63 us
  Pallas kernels: 46.4 us -> 45.9 us
    unnamed x1, local copies, waits for them, and re-layouts: 1.47 us -> 0.63 us
    pallas_call x1, Pallas kernels: 46.4 us -> 45.9 us  [on_device(): pl.pallas_call(functools.partial(kernel, dims), out_shape=pltpu.VMEM((TLA...]
where the time goes in v5:
time: 46.7 us; the launch traced here: 46.5 us
  Pallas kernels  45.9 us (98%)
  local copies, waits for them, and re-layouts  0.63 us (1%)
    pallas_call x1, Pallas kernels, on_device(): pl.pallas_call(functools.partial(kernel, dims), out_shape=pltpu.VMEM((TLA...  45.9 us

profile of v5, /device:TPU:0, one launch (start us, length us, event | category | flops | bytes accessed | tf_op | source)
XLA Modules:
  0.0 46.5 jit_solution(2934667193738626338)
XLA Ops:
  0.0 45.9 %shard_map.127 = bf16[8,16,256]{2,1,0:T(8,128)(2,1)S(1)} custom-call(bf16[31,128,256]{2,1,0:T(8,128)(2,1)} %bitcast.4, f32[128,2,256]{2,1,0:T(2,128)} %offset_hbm.1, s32[128,256]{1,0:T(8,128)} %cell_hbm.1, s32[128,256]{1,0:T(8,128)} %slot_hbm.1, s32[1,128]{1,0:T(1,128)} %count_hbm.1, bf16[384,256]{1,0:T(8,128)(2,1)} %embed_weight_hbm.1, f32[1,256]{1,0:T(1,128)} %bitcast.5, ...), custom_call_target="tpu_custom_call" | custom-call | tf_op jit(solution)/shard_map/pallas_call | solution.py:454
  45.9 0.6 %copy.15 = bf16[8,16,256]{2,1,0:T(8,128)(2,1)} copy(bf16[8,16,256]{2,1,0:T(8,128)(2,1)S(1)} %shard_map.127) | data formatting | bytes 131072

commit v6 on v5

--- a/solution.py
+++ b/solution.py
@@ -82,7 +82,7 @@
         for dy in range(ny)
         if dx or dz or dc or dy
     ]
-    return sorted(offsets, key=lambda o: (o[0] * 37 + o[1] * 59 + o[2] * 83 + o[3] * 101) % 127)
+    return sorted(offsets, key=lambda o: (o[0] * 37 + o[1] * 59 + o[2] * 19 + o[3] * 101) % 127)
 
 
 def kernel(

time: 46.7 us -> 46.4 us (level)
  no operation moved by 1% of the time
where the time goes in v6:
time: 46.4 us; the launch traced here: 46.3 us
  Pallas kernels  45.6 us (98%)
  local copies, waits for them, and re-layouts  0.63 us (1%)
    pallas_call x1, Pallas kernels, on_device(): pl.pallas_call(functools.partial(kernel, dims), out_shape=pltpu.VMEM((TLA...  45.6 us

profile of v6, /device:TPU:0, one launch (start us, length us, event | category | flops | bytes accessed | tf_op | source)
XLA Modules:
  0.0 46.3 jit_solution(4653965070948149878)
XLA Ops:
  0.0 45.6 %shard_map.127 = bf16[8,16,256]{2,1,0:T(8,128)(2,1)S(1)} custom-call(bf16[31,128,256]{2,1,0:T(8,128)(2,1)} %bitcast.4, f32[128,2,256]{2,1,0:T(2,128)} %offset_hbm.1, s32[128,256]{1,0:T(8,128)} %cell_hbm.1, s32[128,256]{1,0:T(8,128)} %slot_hbm.1, s32[1,128]{1,0:T(1,128)} %count_hbm.1, bf16[384,256]{1,0:T(8,128)(2,1)} %embed_weight_hbm.1, f32[1,256]{1,0:T(1,128)} %bitcast.5, ...), custom_call_target="tpu_custom_call" | custom-call | tf_op jit(solution)/shard_map/pallas_call | solution.py:454
  45.6 0.6 %copy.15 = bf16[8,16,256]{2,1,0:T(8,128)(2,1)} copy(bf16[8,16,256]{2,1,0:T(8,128)(2,1)S(1)} %shard_map.127) | data formatting | bytes 131072

commit v7 on v5

--- a/solution.py
+++ b/solution.py
@@ -369,6 +369,8 @@
     for copy in exchange[3:]:
         copy.start()
     framed_ref[:, 2:10, 1] = embedded.reshape(4, 8, 16, D)
+    send_code(pl.ds(1, tiles - 1), pl.ds(1, tiles - 1), 0, partners[0]).wait_send()
+    send_values(pl.ds(1, tiles - 1), pl.ds(1, tiles - 1), 0, partners[0]).wait_send()
     for copy in exchange:
         copy.wait_recv()
 
@@ -420,8 +422,6 @@
 
     for copy in exchange:
         copy.wait_send()
-    send_code(pl.ds(1, tiles - 1), pl.ds(1, tiles - 1), 0, partners[0]).wait_send()
-    send_values(pl.ds(1, tiles - 1), pl.ds(1, tiles - 1), 0, partners[0]).wait_send()
 
 
 def physical(lons, lats):

time: 46.7 us -> 46.7 us (level)
  no operation moved by 1% of the time
where the time goes in v7:
time: 46.7 us; the launch traced here: 46.5 us
  Pallas kernels  45.9 us (98%)
  local copies, waits for them, and re-layouts  0.63 us (1%)
    pallas_call x1, Pallas kernels, on_device(): pl.pallas_call(functools.partial(kernel, dims), out_shape=pltpu.VMEM((TLA...  45.9 us

profile of v7, /device:TPU:0, one launch (start us, length us, event | category | flops | bytes accessed | tf_op | source)
XLA Modules:
  0.0 46.5 jit_solution(13958705038124666563)
XLA Ops:
  0.0 45.9 %shard_map.127 = bf16[8,16,256]{2,1,0:T(8,128)(2,1)S(1)} custom-call(bf16[31,128,256]{2,1,0:T(8,128)(2,1)} %bitcast.4, f32[128,2,256]{2,1,0:T(2,128)} %offset_hbm.1, s32[128,256]{1,0:T(8,128)} %cell_hbm.1, s32[128,256]{1,0:T(8,128)} %slot_hbm.1, s32[1,128]{1,0:T(1,128)} %count_hbm.1, bf16[384,256]{1,0:T(8,128)(2,1)} %embed_weight_hbm.1, f32[1,256]{1,0:T(1,128)} %bitcast.5, ...), custom_call_target="tpu_custom_call" | custom-call | tf_op jit(solution)/shard_map/pallas_call | solution.py:454
  45.9 0.6 %copy.15 = bf16[8,16,256]{2,1,0:T(8,128)(2,1)} copy(bf16[8,16,256]{2,1,0:T(8,128)(2,1)S(1)} %shard_map.127) | data formatting | bytes 131072
